TPU v7x, 512 devices: a whole 4x4x16 slice. The times are simulated.
512 devices in a mesh: slab: 128 (over x, z, core), sub: 4 (over y).
Axes of the slice: x: 4, y: 4, z: 16, core: 2. Of those that a mesh axis runs over, the one named last changes fastest.
Arguments:
- ensemble: float32 [2, 15, 80, 65536], P(None, None, None, ('slab', 'sub')), may hold values from -6 to 6
- obs_value: float32 [2, 256], replicated, may hold values from -6 to 6
- obs_var: float32 [2, 256], replicated, may hold values from 0.5 to 4
- obs_owner: int32 [2, 256, 1], replicated, may hold values from 0 to 127; in each aligned block of 256 rows (0 to 255, 256 to 511, ..., all dimensions but the last counted through in order) at most 8 rows name the same one
- obs_column: int32 [2, 256], replicated, may hold values from 0 to 511
- home_block: int32 [2, 256], replicated, may hold values from -1 to 1
- batch_order: int32 [2], replicated, may hold values from 0 to 1, each once
Outputs:
- analysis: float32 [2, 15, 80, 65536], P(None, None, None, ('slab', 'sub'))
- assimilated_priors: float32 [2, 256, 160], replicated
Inputs may be any that keep to these rules, and one draw needn't show every extreme that they name: `obs_owner`: in each batch no slab owns more than 8 observations; in some batch one slab owns exactly 8. `batch_order`: each batch appears once.
All inputs are finite; a program needn't handle non-finite values.
Results may differ from a plain program's by a relative error of at most 0.00012.
Values sent between devices are 32-bit elements; how exact they have to be, the bound alone decides.
A program may use at most 64 MiB of HBM per device.

v0:
```python
import jax
import jax.numpy as jnp
from jax import lax
from jax.sharding import PartitionSpec as P

BANDS = 2
BLK = 16
BATCHES = 2
CAP = 8
HIGHEST = lax.Precision.HIGHEST


def gc_weight(first, second, nblocks, length):
    block_gap = jnp.abs(first - second)
    block_gap = jnp.minimum(block_gap, nblocks - block_gap)
    scaled_gap = block_gap.astype(jnp.float32) / length
    near_part = (
        ((-0.25 * scaled_gap + 0.5) * scaled_gap + 0.625) * scaled_gap**3
        - 5.0 / 3.0 * scaled_gap**2
        + 1.0
    )
    floored = jnp.maximum(scaled_gap, 1.0)
    far_part = (
        (
            (((scaled_gap / 12.0 - 0.5) * scaled_gap + 0.625) * scaled_gap + 5.0 / 3.0) * scaled_gap
            - 5.0
        )
        * scaled_gap
        + 4.0
        - 2.0 / (3.0 * floored)
    )
    return jnp.where(scaled_gap <= 1.0, near_part, jnp.where(scaled_gap < 2.0, far_part, 0.0))


def obs_statistics(current, values, variances, members):
    banded = current.reshape(current.shape[0], BANDS, members)
    whole_obs = jnp.sum(banded, axis=1)
    centre = jnp.mean(whole_obs, axis=1, keepdims=True)
    spread = jnp.sum((whole_obs - centre) ** 2, axis=1) / (members - 1) + 1e-06
    post_var = 1.0 / (1.0 / spread + 1.0 / variances)
    post_mean = post_var * (centre[:, 0] / spread + values / variances)
    increments = (post_mean - centre[:, 0])[:, None] + (jnp.sqrt(post_var / spread) - 1.0)[
        :, None
    ] * (whole_obs - centre)
    deviations = banded - jnp.mean(banded, axis=2, keepdims=True)
    return (deviations, spread, increments)


def update_pool(prior_pool, pool_homes, deviations, spread, increments, obs_homes, nblocks, decays):
    members = deviations.shape[2]
    banded = prior_pool.reshape(prior_pool.shape[0], prior_pool.shape[1], BANDS, members)
    new_bands = []
    for band_no in range(BANDS):
        pool_band = banded[:, :, band_no, :]
        pool_dev = pool_band - jnp.mean(pool_band, axis=2, keepdims=True)
        weights = (
            gc_weight(pool_homes[:, :, None], obs_homes[None, None, :], nblocks, decays[band_no])
            / ((members - 1) * spread)[None, None, :]
        )
        crossed = jnp.einsum("bpm,km->bpk", pool_dev, deviations[:, band_no, :], precision=HIGHEST)
        change = jnp.einsum("bpk,km->bpm", crossed * weights, increments, precision=HIGHEST)
        new_bands.append(pool_band + change)
    return jnp.stack(new_bands, axis=2).reshape(prior_pool.shape)


def update_state(ensemble, my_cols, deviations, spread, increments, obs_homes, nblocks, decays):
    members = ensemble.shape[2]
    new_bands = []
    for band_no in range(BANDS):
        band_layer = ensemble[band_no]
        layer_dev = band_layer - jnp.mean(band_layer, axis=1, keepdims=True)
        obs_dev = deviations[:, band_no, :]
        weights = (
            gc_weight((my_cols // BLK)[:, None], obs_homes[None, :], nblocks, decays[band_no])
            / ((members - 1) * spread)[None, :]
        )

        def one_level(level_dev):
            crossed = jnp.einsum("mc,km->ck", level_dev, obs_dev, precision=HIGHEST)
            return jnp.einsum("ck,km->mc", crossed * weights, increments, precision=HIGHEST)

        change = lax.map(one_level, layer_dev)
        new_bands.append(band_layer + change)
    return jnp.stack(new_bands, axis=0)


def slot_table(owners, slot_rank, slab_number, capacity):
    obs_count = owners.shape[1]
    matches = (owners == slab_number)[:, None, :] & (
        slot_rank[:, None, :] == jnp.arange(capacity, dtype=jnp.int32)[None, :, None]
    )
    slot_obs = jnp.sum(
        jnp.where(matches, jnp.arange(obs_count, dtype=jnp.int32)[None, None, :], 0), axis=2
    )
    slot_valid = jnp.any(matches, axis=2)
    return (slot_obs, slot_valid)


def per_device(ensemble, obs_value, obs_var, obs_owner, obs_column, home_block, batch_order):
    members = ensemble.shape[2]
    levels_count = ensemble.shape[1]
    cols_dev = ensemble.shape[3]
    slab_count = lax.axis_size("slab")
    sub_count = lax.axis_size("sub")
    slab_index = lax.axis_index("slab")
    sub_index = lax.axis_index("sub")
    obs_batch = obs_value.shape[1]
    capacity = CAP
    cols_slab = cols_dev * sub_count
    nblocks = cols_slab * slab_count // BLK
    span_broad = cols_slab // (4 * BLK)
    span_narrow = max(span_broad // 4, 1)
    decays = (float(span_broad), float(span_narrow))
    owners = obs_owner[:, :, 0]
    obs_home = jnp.mod((owners * cols_slab + obs_column) // BLK + home_block, nblocks)
    onehot = (owners[:, :, None] == jnp.arange(slab_count, dtype=jnp.int32)[None, None, :]).astype(
        jnp.int32
    )
    running = jnp.cumsum(onehot, axis=1) - 1
    slot_rank = jnp.sum(onehot * running, axis=2)
    slot_global = owners * capacity + slot_rank
    slot_obs, slot_valid = slot_table(owners, slot_rank, slab_index, capacity)
    slot_column = jnp.take_along_axis(obs_column, slot_obs, axis=1)
    slot_level = slot_obs % levels_count
    holder = slot_column // cols_dev
    local_col = slot_column % cols_dev
    picked = ensemble[:, slot_level, :, local_col]
    retain = slot_valid & (holder == sub_index)
    picked = jnp.where(retain[:, :, None, None], picked, 0.0).reshape(
        BATCHES, capacity, BANDS * members
    )
    slot_priors = lax.psum(picked, "sub")
    slot_homes = jnp.take_along_axis(obs_home, slot_obs, axis=1)
    my_cols = (slab_index * sub_count + sub_index) * cols_dev + jnp.arange(
        cols_dev, dtype=jnp.int32
    )
    recorded = jnp.zeros((BATCHES, obs_batch, BANDS * members), jnp.float32)
    for step_no in range(BATCHES):
        batch_id = batch_order[step_no]
        own_slots = slot_priors[batch_id]
        values = obs_value[batch_id]
        variances = obs_var[batch_id]
        obs_homes = obs_home[batch_id]
        gathered = lax.all_gather(own_slots, "slab", axis=0, tiled=True)
        current = gathered[slot_global[batch_id]]
        live = jnp.ones((obs_batch,), jnp.bool_)
        recorded = recorded.at[batch_id].set(current)
        deviations, spread, increments = obs_statistics(current, values, variances, members)
        increments = jnp.where(live[:, None], increments, 0.0)
        slot_priors = update_pool(
            slot_priors, slot_homes, deviations, spread, increments, obs_homes, nblocks, decays
        )
        ensemble = update_state(
            ensemble, my_cols, deviations, spread, increments, obs_homes, nblocks, decays
        )
    return (ensemble, recorded)


def solution(mesh):
    placed = (P(None, None, None, ("slab", "sub")), P(), P(), P(), P(), P(), P())
    return jax.shard_map(
        per_device,
        mesh=mesh,
        in_specs=placed,
        out_specs=(P(None, None, None, ("slab", "sub")), P()),
        check_vma=False,
    )
```

profile of v0, /device:TPU:1, one launch (start us, length us, event | category | flops | bytes accessed | tf_op | source)
XLA Modules:
  0.0 351.5 jit_solution(10229613459352276190)
XLA Ops:
  5.6 14.3 %psum.7 = f32[2,8,160]{2,1,0:T(8,128)S(1)} all-reduce(f32[2,8,160]{2,1,0:T(8,128)S(1)} %broadcast_select_fusion), channel_id=1, replica_groups=mesh['slab'=128,'sub'=4] {'sub'}, use_global_device_ids=true, to_apply=%region_6.8 | all-reduce | flops 2560 | bytes 20480 | tf_op jit(solution)/shard_map/psum | solution.py:132
  22.5 111.6 %all-gather = f32[1,1024,160]{2,1,0:T(8,128)S(1)} all-gather(f32[1,8,160]{2,1,0:T(8,128)S(1)} %constant_dynamic-slice_fusion.9), channel_id=2, replica_groups=mesh['slab'=128,'sub'=4] {'slab'}, dimensions={1}, use_global_device_ids=true | all-gather | bytes 660480 | tf_op jit(solution)/shard_map/all_gather | solution.py:144
  139.6 99.9 %all-gather.1 = f32[1,1024,160]{2,1,0:T(8,128)S(1)} all-gather(f32[1,8,160]{2,1,0:T(8,128)S(1)} %constant_dynamic-slice_fusion.4), channel_id=3, replica_groups=mesh['slab'=128,'sub'=4] {'slab'}, dimensions={1}, use_global_device_ids=true | all-gather | bytes 660480 | tf_op jit(solution)/shard_map/all_gather | solution.py:144
  245.5 24.5 %while.48 = (s32[]{:T(128)}, f32[15,80,128]{2,1,0:T(8,128)S(1)}, f32[15,80,128]{2,1,0:T(8,128)}, f32[256,80]{1,0:T(8,128)S(1)}, f32[256,80]{1,0:T(8,128)S(1)}, /...) while((s32[]{:T(128)}, f32[15,80,128]{2,1,0:T(8,128)S(1)}, ...), condition=%wide.region_24.26_spmd.clone, body=%wide.region_23.25_spmd.clone.sunk | while | flops 64094208 | bytes 560225 | solution.py:82
  245.5 1.2 convolution_multiply_fusion.12
  247.2 1.2 convolution_multiply_fusion.12
  248.8 1.2 convolution_multiply_fusion.12
  250.4 1.2 convolution_multiply_fusion.12
  252.1 1.2 convolution_multiply_fusion.12
  253.7 1.2 convolution_multiply_fusion.12
  255.3 1.2 convolution_multiply_fusion.12
  257.0 1.2 convolution_multiply_fusion.12
  258.6 1.2 convolution_multiply_fusion.12
  260.2 1.2 convolution_multiply_fusion.12
  261.9 1.2 convolution_multiply_fusion.12
  263.5 1.2 convolution_multiply_fusion.12
  265.1 1.2 convolution_multiply_fusion.12
  266.8 1.2 convolution_multiply_fusion.12
  268.4 1.2 convolution_multiply_fusion.12
  270.8 26.6 %while.46 = (s32[]{:T(128)}, f32[15,80,128]{2,1,0:T(8,128)S(1)}, f32[15,80,128]{2,1,0:T(8,128)S(1)}, f32[256,80]{1,0:T(8,128)}, f32[256,80]{1,0:T(8,128)S(1)}, /...) while((s32[]{:T(128)}, f32[15,80,128]{2,1,0:T(8,128)S(1)}, ...), condition=%wide.region_12.14_spmd.clone, body=%wide.region_11.13_spmd.clone.sunk | while | flops 64094208 | bytes 559717 | solution.py:82
  270.8 1.4 convolution_multiply_fusion.10
  272.6 1.4 convolution_multiply_fusion.10
  274.4 1.4 convolution_multiply_fusion.10
  276.2 1.4 convolution_multiply_fusion.10
  277.9 1.4 convolution_multiply_fusion.10
  279.7 1.4 convolution_multiply_fusion.10
  281.5 1.4 convolution_multiply_fusion.10
  283.3 1.4 convolution_multiply_fusion.10
  285.0 1.4 convolution_multiply_fusion.10
  286.8 1.4 convolution_multiply_fusion.10
  288.6 1.4 convolution_multiply_fusion.10
  290.3 1.4 convolution_multiply_fusion.10
  292.1 1.4 convolution_multiply_fusion.10
  293.9 1.4 convolution_multiply_fusion.10
  295.7 1.4 convolution_multiply_fusion.10
  299.0 24.5 %while.49 = (s32[]{:T(128)}, f32[15,80,128]{2,1,0:T(8,128)S(1)}, f32[15,80,128]{2,1,0:T(8,128)}, f32[256,80]{1,0:T(8,128)S(1)}, f32[256,80]{1,0:T(8,128)S(1)}, /...) while((s32[]{:T(128)}, f32[15,80,128]{2,1,0:T(8,128)S(1)}, ...), condition=%wide.region_27.29_spmd.clone, body=%wide.region_26.28_spmd.clone.sunk | while | flops 64094208 | bytes 560225 | solution.py:82
  300.6 1.2 convolution_multiply_fusion.13
  302.3 1.2 convolution_multiply_fusion.13
  303.9 1.2 convolution_multiply_fusion.13
  305.5 1.2 convolution_multiply_fusion.13
  307.2 1.2 convolution_multiply_fusion.13
  310.4 1.2 convolution_multiply_fusion.13
  312.1 1.2 convolution_multiply_fusion.13
  315.3 1.2 convolution_multiply_fusion.13
  317.0 1.2 convolution_multiply_fusion.13
  320.3 1.2 convolution_multiply_fusion.13
  321.9 1.2 convolution_multiply_fusion.13
  324.4 24.6 %while.47 = (s32[]{:T(128)}, f32[15,80,128]{2,1,0:T(8,128)S(1)}, f32[15,80,128]{2,1,0:T(8,128)}, f32[256,80]{1,0:T(8,128)S(1)}, f32[256,80]{1,0:T(8,128)S(1)}, /...) while((s32[]{:T(128)}, f32[15,80,128]{2,1,0:T(8,128)S(1)}, ...), condition=%wide.region_21.23_spmd.clone, body=%wide.region_20.22_spmd.clone.sunk | while | flops 64094208 | bytes 560225 | solution.py:82
  324.4 1.2 convolution_multiply_fusion.11
  326.0 1.2 convolution_multiply_fusion.11
  327.7 1.2 convolution_multiply_fusion.11
  329.3 1.2 convolution_multiply_fusion.11
  331.0 1.2 convolution_multiply_fusion.11
  332.6 1.2 convolution_multiply_fusion.11
  334.2 1.2 convolution_multiply_fusion.11
  335.9 1.2 convolution_multiply_fusion.11
  337.5 1.2 convolution_multiply_fusion.11
  339.2 1.2 convolution_multiply_fusion.11
  340.8 1.2 convolution_multiply_fusion.11
  342.4 1.2 convolution_multiply_fusion.11
  344.1 1.2 convolution_multiply_fusion.11
  345.7 1.2 convolution_multiply_fusion.11
  347.3 1.2 convolution_multiply_fusion.11
  349.0 1.3 add_bitcast_fusion.1
  (188 shorter events, 46.3 us)
Async XLA Ops:
  0.6 1.6 copy-start.3
  0.6 2.1 copy-start
  2.0 1.8 copy-start.1
  3.8 16.2 %copy-start.4 = (s32[2]{0:T(128)S(1)}, s32[2]{0:T(128)}, u32[]{:S(2)}) copy-start(s32[2]{0:T(128)} %param.27) | copy-start | bytes 28
  4.8 131.3 %copy-start.5 = (s32[2,256]{1,0:T(2,128)S(1)}, s32[2,256]{1,0:T(2,128)}, u32[]{:S(2)}) copy-start(s32[2,256]{1,0:T(2,128)} %param.26) | copy-start | bytes 6148
  136.2 1.3 copy-start.6
  136.2 1.3 copy-start.7
  137.5 2.0 copy-start.8
  137.8 101.7 %copy-start.10 = (s32[1,256]{1,0:T(1,128)}, s32[1,256]{1,0:T(1,128)S(1)}, u32[]{:S(2)}) copy-start(s32[1,256]{1,0:T(1,128)S(1)} %get-tuple-element.436) | copy-start | bytes 3076
  239.5 1.0 copy-start.12
  244.5 1.0 copy-start.9
  244.5 1.0 copy-start.11
  270.0 0.8 copy-start.13
  297.7 1.3 copy-start.14
  323.5 0.8 copy-start.2
where the time goes:
time: 355 us; the launch traced here: 352 us
  blocking collectives  226 us (64%)
  matrix products  99.2 us (28%)
  local copies, waits for them, and re-layouts  10.4 us (3%)
  other arithmetic  9.13 us (3%)
  between operations  5.16 us (1%)
    all_gather x2, blocking collectives, per_device(): gathered = lax.all_gather(own_slots, 'slab', axis=0, tiled=True)  212 us
    dot_general x60, matrix products, one_level(): crossed = jnp.einsum('mc,km->ck', level_dev, obs_dev, precision=HIGHEST)  76 us
    dot_general x60, matrix products, one_level(): jnp.einsum('ck,km->mc', crossed * weights, increments, precision=HIGHEST)  22.5 us
    psum x1, blocking collectives, per_device(): slot_priors = lax.psum(picked, 'sub')  14.3 us

commit v1 on v0

--- a/solution.py
+++ b/solution.py
@@ -8,6 +8,13 @@
 BATCHES = 2
 CAP = 8
 HIGHEST = lax.Precision.HIGHEST
+
+
+def swapped_in(x, name, dim):
+    devices = lax.axis_size(name)
+    blocks = jnp.stack([x for _ in range(devices)])
+    blocks = lax.all_to_all(blocks, name, split_axis=0, concat_axis=0)
+    return jnp.concatenate(blocks, axis=dim)
 
 
 def gc_weight(first, second, nblocks, length):
@@ -141,7 +148,7 @@
         values = obs_value[batch_id]
         variances = obs_var[batch_id]
         obs_homes = obs_home[batch_id]
-        gathered = lax.all_gather(own_slots, "slab", axis=0, tiled=True)
+        gathered = swapped_in(own_slots, "slab", 0)
         current = gathered[slot_global[batch_id]]
         live = jnp.ones((obs_batch,), jnp.bool_)
         recorded = recorded.at[batch_id].set(current)

time: 355 us -> 230 us (0.65)
  blocking collectives: 226 us -> 14.3 us
  waiting for transfers between devices: 0 us -> 49.3 us
  starting transfers between devices: 0 us -> 32.3 us
  local copies, waits for them, and re-layouts: 10.4 us -> 14.7 us
    all_gather x2 -> x0, blocking collectives: 212 us -> none  [per_device(): gathered = lax.all_gather(own_slots, 'slab', axis=0, tiled=True)]
    all_to_all x0 -> x2, waiting for transfers between devices: none -> 49.3 us  [swapped_in(): blocks = lax.all_to_all(blocks, name, split_axis=0, concat_axis=0)]
    all_to_all x0 -> x2, starting transfers between devices: none -> 32.3 us  [swapped_in(): blocks = lax.all_to_all(blocks, name, split_axis=0, concat_axis=0)]
  transfers between devices with their start and end apart: 0 -> 2, of which waited for: 0 -> 1; matrix products, arithmetic and copies ran while one was open for 0% -> 25% of each run, Pallas kernels for 0% -> 0%
where the time goes in v1:
time: 230 us; the launch traced here: 226 us
  matrix products  99.1 us (43%)
  waiting for transfers between devices  49.3 us (21%)
  starting transfers between devices  32.3 us (14%)
  local copies, waits for them, and re-layouts  14.7 us (6%)
  blocking collectives  14.3 us (6%)
  other arithmetic  9.16 us (4%)
  between operations  5.08 us (2%)
    dot_general x60, matrix products, one_level(): crossed = jnp.einsum('mc,km->ck', level_dev, obs_dev, precision=HIGHEST)  75.8 us
    all_to_all x2, waiting for transfers between devices, swapped_in(): blocks = lax.all_to_all(blocks, name, split_axis=0, concat_axis=0)  49.3 us
    all_to_all x2, starting transfers between devices, swapped_in(): blocks = lax.all_to_all(blocks, name, split_axis=0, concat_axis=0)  32.3 us
    dot_general x60, matrix products, one_level(): jnp.einsum('ck,km->mc', crossed * weights, increments, precision=HIGHEST)  22.6 us
    psum x1, blocking collectives, per_device(): slot_priors = lax.psum(picked, 'sub')  14.3 us
    unnamed x31, local copies, waits for them, and re-layouts  4.95 us
  transfers between devices with their start and end apart: 2, of which 1 were waited for; matrix products, arithmetic and copies ran while one was open for 25% of the time, Pallas kernels for 0%

profile of v1, /device:TPU:1, one launch (start us, length us, event | category | flops | bytes accessed | tf_op | source)
XLA Modules:
  0.0 225.8 jit_solution(542486844694275009)
XLA Ops:
  6.3 14.3 %psum.7 = f32[2,8,160]{2,1,0:T(8,128)S(1)} all-reduce(f32[2,8,160]{2,1,0:T(8,128)S(1)} %broadcast_select_fusion), channel_id=1, replica_groups=mesh['slab'=128,'sub'=4] {'sub'}, use_global_device_ids=true, to_apply=%region_6.8 | all-reduce | flops 2560 | bytes 20480 | tf_op jit(solution)/shard_map/psum | solution.py:139
  24.2 23.3 %all-to-all-start = ((f32[128,8,160]{2,1,0:T(8,128)}), f32[128,8,160]{2,1,0:T(8,128)S(1)}, u32[]{:S(2)}, u32[]{:S(2)}) async-start(f32[128,8,160]{2,1,0:T(8,128)} %stack.24), calls=%async_computation | async-start | bytes 2097152 | tf_op jit(solution)/shard_map/all_to_all | solution.py:16
  52.6 49.3 %all-to-all-done = f32[128,8,160]{2,1,0:T(8,128)S(1)} async-done(((f32[128,8,160]{2,1,0:T(8,128)}), f32[128,8,160]{2,1,0:T(8,128)S(1)}, u32[]{:S(2)}, u32[]{:S(2)}) %all-to-all-start) | async-done | bytes 655392 | tf_op jit(solution)/shard_map/all_to_all | solution.py:16
  105.3 9.0 %all-to-all-start.1 = ((f32[128,8,160]{2,1,0:T(8,128)}), f32[128,8,160]{2,1,0:T(8,128)}, u32[]{:S(2)}, u32[]{:S(2)}) async-start(f32[128,8,160]{2,1,0:T(8,128)} %stack.28), calls=%async_computation.1 | async-start | bytes 2097152 | tf_op jit(solution)/shard_map/all_to_all | solution.py:16
  114.5 24.6 %while.48 = (s32[]{:T(128)}, f32[15,80,128]{2,1,0:T(8,128)S(1)}, f32[15,80,128]{2,1,0:T(8,128)}, f32[256,80]{1,0:T(8,128)S(1)}, f32[256,80]{1,0:T(8,128)S(1)}, /...) while((s32[]{:T(128)}, f32[15,80,128]{2,1,0:T(8,128)S(1)}, ...), condition=%wide.region_24.26_spmd.clone, body=%wide.region_23.25_spmd.clone.sunk | while | flops 64094208 | bytes 560225 | solution.py:89
  116.1 1.2 convolution_multiply_fusion.12
  117.7 1.2 convolution_multiply_fusion.12
  119.4 1.2 convolution_multiply_fusion.12
  121.0 1.2 convolution_multiply_fusion.12
  122.7 1.2 convolution_multiply_fusion.12
  124.3 1.2 convolution_multiply_fusion.12
  125.9 1.2 convolution_multiply_fusion.12
  127.6 1.2 convolution_multiply_fusion.12
  129.2 1.2 convolution_multiply_fusion.12
  130.8 1.2 convolution_multiply_fusion.12
  132.5 1.2 convolution_multiply_fusion.12
  134.1 1.2 convolution_multiply_fusion.12
  135.8 1.2 convolution_multiply_fusion.12
  137.4 1.2 convolution_multiply_fusion.12
  139.8 26.5 %while.46 = (s32[]{:T(128)}, f32[15,80,128]{2,1,0:T(8,128)S(1)}, f32[15,80,128]{2,1,0:T(8,128)S(1)}, f32[256,80]{1,0:T(8,128)}, f32[256,80]{1,0:T(8,128)S(1)}, /...) while((s32[]{:T(128)}, f32[15,80,128]{2,1,0:T(8,128)S(1)}, ...), condition=%wide.region_12.14_spmd.clone, body=%wide.region_11.13_spmd.clone.sunk | while | flops 64094208 | bytes 559717 | solution.py:89
  139.8 1.4 convolution_multiply_fusion.10
  141.6 1.4 convolution_multiply_fusion.10
  143.4 1.4 convolution_multiply_fusion.10
  145.1 1.4 convolution_multiply_fusion.10
  146.9 1.4 convolution_multiply_fusion.10
  148.7 1.4 convolution_multiply_fusion.10
  150.4 1.4 convolution_multiply_fusion.10
  152.2 1.4 convolution_multiply_fusion.10
  154.0 1.4 convolution_multiply_fusion.10
  155.7 1.4 convolution_multiply_fusion.10
  157.5 1.4 convolution_multiply_fusion.10
  159.2 1.4 convolution_multiply_fusion.10
  161.0 1.4 convolution_multiply_fusion.10
  162.8 1.4 convolution_multiply_fusion.10
  164.5 1.4 convolution_multiply_fusion.10
  167.5 1.3 broadcast_subtract_fusion.1
  168.8 2.2 gather_fusion.2
  173.2 24.5 %while.49 = (s32[]{:T(128)}, f32[15,80,128]{2,1,0:T(8,128)S(1)}, f32[15,80,128]{2,1,0:T(8,128)}, f32[256,80]{1,0:T(8,128)S(1)}, f32[256,80]{1,0:T(8,128)S(1)}, /...) while((s32[]{:T(128)}, f32[15,80,128]{2,1,0:T(8,128)S(1)}, ...), condition=%wide.region_27.29_spmd.clone, body=%wide.region_26.28_spmd.clone.sunk | while | flops 64094208 | bytes 560225 | solution.py:89
  174.9 1.2 convolution_multiply_fusion.13
  176.5 1.2 convolution_multiply_fusion.13
  179.8 1.2 convolution_multiply_fusion.13
  181.4 1.2 convolution_multiply_fusion.13
  184.7 1.2 convolution_multiply_fusion.13
  186.3 1.2 convolution_multiply_fusion.13
  189.6 1.2 convolution_multiply_fusion.13
  191.2 1.2 convolution_multiply_fusion.13
  194.5 1.2 convolution_multiply_fusion.13
  196.1 1.2 convolution_multiply_fusion.13
  198.6 24.6 %while.47 = (s32[]{:T(128)}, f32[15,80,128]{2,1,0:T(8,128)S(1)}, f32[15,80,128]{2,1,0:T(8,128)}, f32[256,80]{1,0:T(8,128)S(1)}, f32[256,80]{1,0:T(8,128)S(1)}, /...) while((s32[]{:T(128)}, f32[15,80,128]{2,1,0:T(8,128)S(1)}, ...), condition=%wide.region_21.23_spmd.clone, body=%wide.region_20.22_spmd.clone.sunk | while | flops 64094208 | bytes 560225 | solution.py:89
  200.3 1.2 convolution_multiply_fusion.11
  201.9 1.2 convolution_multiply_fusion.11
  203.6 1.2 convolution_multiply_fusion.11
  205.2 1.2 convolution_multiply_fusion.11
  206.8 1.2 convolution_multiply_fusion.11
  208.5 1.2 convolution_multiply_fusion.11
  210.1 1.2 convolution_multiply_fusion.11
  211.8 1.2 convolution_multiply_fusion.11
  213.4 1.2 convolution_multiply_fusion.11
  215.0 1.2 convolution_multiply_fusion.11
  216.7 1.2 convolution_multiply_fusion.11
  218.3 1.2 convolution_multiply_fusion.11
  220.0 1.2 convolution_multiply_fusion.11
  221.6 1.2 convolution_multiply_fusion.11
  223.2 1.3 add_bitcast_fusion.1
  (184 shorter events, 50.9 us)
Async XLA Ops:
  0.6 2.2 copy-start.3
  0.6 2.9 %copy-start = (s32[2,256]{1,0:T(2,128)S(1)}, s32[2,256]{1,0:T(2,128)}, u32[]{:S(2)}) copy-start(s32[2,256]{1,0:T(2,128)} %param.25) | copy-start | bytes 6148
  2.7 1.8 copy-start.1
  4.4 16.2 %copy-start.4 = (s32[2]{0:T(128)S(1)}, s32[2]{0:T(128)}, u32[]{:S(2)}) copy-start(s32[2]{0:T(128)} %param.27) | copy-start | bytes 28
  24.2 24.7 %copy-start.5 = (s32[2,256]{1,0:T(2,128)S(1)}, s32[2,256]{1,0:T(2,128)}, u32[]{:S(2)}) copy-start(s32[2,256]{1,0:T(2,128)} %param.26) | copy-start | bytes 6148
  24.2 26.5 %copy-start.6 = (f32[2,256]{1,0:T(2,128)S(1)}, f32[2,256]{1,0:T(2,128)}, u32[]{:S(2)}) copy-start(f32[2,256]{1,0:T(2,128)} %param.22) | copy-start | bytes 6148
  24.2 26.5 %copy-start.7 = (f32[2,256]{1,0:T(2,128)S(1)}, f32[2,256]{1,0:T(2,128)}, u32[]{:S(2)}) copy-start(f32[2,256]{1,0:T(2,128)} %param.23) | copy-start | bytes 6148
  24.2 26.5 %copy-start.8 = (s32[3]{0:T(128)S(1)}, s32[3]{0:T(128)}, u32[]{:S(2)}) copy-start(s32[3]{0:T(128)} %constant.293.clone.1) | copy-start | bytes 40
  24.2 77.7 %all-to-all-start = ((f32[128,8,160]{2,1,0:T(8,128)}), f32[128,8,160]{2,1,0:T(8,128)S(1)}, u32[]{:S(2)}, u32[]{:S(2)}) async-start(f32[128,8,160]{2,1,0:T(8,128)} %stack.24), calls=%async_computation | async-start | bytes 2097152 | tf_op jit(solution)/shard_map/all_to_all | solution.py:16
  105.3 63.4 %all-to-all-start.1 = ((f32[128,8,160]{2,1,0:T(8,128)}), f32[128,8,160]{2,1,0:T(8,128)}, u32[]{:S(2)}, u32[]{:S(2)}) async-start(f32[128,8,160]{2,1,0:T(8,128)} %stack.28), calls=%async_computation.1 | async-start | bytes 2097152 | tf_op jit(solution)/shard_map/all_to_all | solution.py:16
  166.3 0.5 copy-start.9
  172.6 0.6 copy-start.10
  197.8 0.8 copy-start.2
